TPU v7x, 256 devices: a whole 4x4x8 slice. The times are simulated.
256 devices in a mesh: row: 16 (over z_lo, x), col: 16 (over y, z_hi, core).
Axes of the slice: x: 4, y: 4, z: 8 (z_hi: 2, z_lo: 4; z = z_hi * 4 + z_lo), core: 2. Of those that a mesh axis runs over, the one named last changes fastest.
Arguments:
- homolog_matrix: bfloat16 [128, 1280, 64], P('row', 'col'), may hold values from -6 to 6
- contact_matrix: bfloat16 [1280, 1280, 128], P('row', 'col'), may hold values from -24 to 24
- genuine_homolog_total: int32 [1], replicated, may hold values from 1 to 128
- genuine_chain_length: int32 [1], replicated, may hold values from 640 to 1280
- tensor_product_matrices: bfloat16 [1, 64, 64], replicated, may hold values from -0.75 to 0.75
- tensor_product_final: bfloat16 [1, 1024, 128], replicated, may hold values from -0.75 to 0.75
- mixing_value_gate_matrix: bfloat16 [1, 64, 512], replicated, may hold values from -0.75 to 0.75
- mixing_logit_matrix: bfloat16 [1, 128, 8], replicated
- mixing_final_matrix: bfloat16 [1, 256, 64], replicated, may hold values from -1.5 to 1.5
- feedforward_gate_expand: bfloat16 [1, 128, 1024], replicated, may hold values from -0.5 to 0.5
- feedforward_shrink_matrix: bfloat16 [1, 512, 128], replicated, may hold values from -0.25 to 0.25
Outputs:
- msa_out: bfloat16 [128, 1280, 64], P('row', 'col')
- pair_out: bfloat16 [1280, 1280, 128], P('row', 'col')
Inputs may be any that keep to these rules, and one draw needn't show every extreme that they name: Sequences from genuine_homolog_total on are padding. Residues from genuine_chain_length on are padding.
All inputs are finite; a program needn't handle non-finite values.
Results may differ from a plain program's by a relative error of at most 0.0065.
The roundings to bfloat16 on the way count: a program that leaves them out, or rounds other values in their place, can miss the bound.
Values may be sent and summed in bfloat16 or wider, within the bound.
No kernel may reach another device: no remote copies, remote signals or barrier semaphores. Data moves between devices by JAX's collectives and lax.ppermute only.
A program may use at most 64 MiB of HBM per device.

v0:
```python
import jax
import jax.numpy as jnp
from jax import lax
from jax.sharding import PartitionSpec as P

EPSILON = 1e-05
MASKED = -1000000000.0


def in_order(parts, dim):
    parts = jnp.moveaxis(parts, 0, dim)
    lengths = parts.shape
    return parts.reshape(*lengths[:dim], lengths[dim] * lengths[dim + 1], *lengths[dim + 2 :])


def from_everyone(value, axis):
    count = lax.axis_size(axis)
    return lax.all_to_all(
        jnp.broadcast_to(value[None], (count, *value.shape)), axis, 0, 0, tiled=True
    )


def gather_directly(value, axis, dim):
    return in_order(from_everyone(value, axis), dim)


def picked(value, axis, root):
    return lax.dynamic_index_in_dim(lax.all_gather(value, axis), root, 0, keepdims=False)


def of_everyone(value, axis):
    everything = from_everyone(value, axis)
    return jnp.max(everything, axis=0)


def over_copies(value, axis):
    return from_everyone(value, axis).sum(axis=0)


def standardize_features(field):
    field = field.astype(jnp.float32)
    center = field - jnp.mean(field, axis=-1, keepdims=True)
    spread = jnp.mean(center * center, axis=-1, keepdims=True)
    return center * lax.rsqrt(spread + EPSILON)


def local(
    homolog_matrix,
    contact_matrix,
    genuine_homolog_total,
    genuine_chain_length,
    tensor_product_matrices,
    tensor_product_final,
    mixing_value_gate_matrix,
    mixing_logit_matrix,
    mixing_final_matrix,
    feedforward_gate_expand,
    feedforward_shrink_matrix,
):
    homolog_rows_local, chain_positions_local, homolog_rows_full = homolog_matrix.shape
    rows_dev = contact_matrix.shape[0]
    pair_width = contact_matrix.shape[2]
    outer_width = tensor_product_matrices.shape[2] // 2
    head_count = mixing_logit_matrix.shape[2]
    hidden_width = mixing_final_matrix.shape[1]
    head_width = hidden_width // head_count
    trans_width = feedforward_shrink_matrix.shape[1]
    row_blocks = rows_dev // 8
    row_index = lax.axis_index("row")
    col_index = lax.axis_index("col")
    ratio = lax.axis_size("row") // lax.axis_size("col")
    total_seqs = homolog_rows_local * lax.axis_size("row")
    seq_ids = row_index * homolog_rows_local + jnp.arange(homolog_rows_local, dtype=jnp.int32)
    res_ids = col_index * chain_positions_local + jnp.arange(chain_positions_local, dtype=jnp.int32)
    pair_ids = row_index * rows_dev + jnp.arange(rows_dev, dtype=jnp.int32)
    seq_float = (seq_ids < genuine_homolog_total[0]).astype(jnp.float32)
    res_valid = res_ids < genuine_chain_length[0]
    res_float = res_valid.astype(jnp.float32)
    row_float = (pair_ids < genuine_chain_length[0]).astype(jnp.float32)
    divisor = jnp.maximum(
        genuine_homolog_total[0].astype(jnp.float32) * row_float[:, None] * res_float[None, :], 1.0
    )
    starts = jnp.arange(row_blocks, dtype=jnp.int32) * 8
    standardized_source = standardize_features(homolog_matrix).astype(jnp.bfloat16)
    reshaped_tensor = standardized_source.reshape(
        homolog_rows_local * chain_positions_local, homolog_rows_full
    )
    projected = jnp.dot(
        reshaped_tensor, tensor_product_matrices[0], preferred_element_type=jnp.float32
    ).reshape(homolog_rows_local, chain_positions_local, 2 * outer_width)
    projected = (projected * (seq_float[:, None, None] * res_float[None, :, None])).astype(
        jnp.bfloat16
    )
    packed = projected.reshape(homolog_rows_local, chain_positions_local * 2 * outer_width)
    columns = gather_directly(packed, "row", 0).reshape(
        total_seqs, chain_positions_local, 2 * outer_width
    )
    left_all = columns[:, :, :outer_width].reshape(total_seqs, chain_positions_local * outer_width)
    right = columns[:, :, outer_width:].reshape(total_seqs, chain_positions_local * outer_width)
    left_cols = picked(left_all, "col", row_index // ratio).reshape(
        total_seqs, chain_positions_local, outer_width
    )
    outer_weight = tensor_product_final[0]

    def outer_rows(inputs):
        start, pair_rows = inputs
        rows = lax.dynamic_slice_in_dim(left_cols, start, 8, 1).reshape(total_seqs, 8 * outer_width)
        product = lax.dot_general(
            rows, right, (((0,), (0,)), ((), ())), preferred_element_type=jnp.float32
        )
        product = product.reshape(8, outer_width, chain_positions_local, outer_width).transpose(
            0, 2, 1, 3
        )
        product = product.reshape(8, chain_positions_local, outer_width * outer_width)
        scale = lax.dynamic_slice_in_dim(divisor, start, 8, 0)
        outer = (product / scale[:, :, None]).astype(jnp.bfloat16)
        update = jnp.dot(
            outer.reshape(8 * chain_positions_local, outer_width * outer_width),
            outer_weight,
            preferred_element_type=jnp.float32,
        )
        return (
            pair_rows.astype(jnp.float32) + update.reshape(8, chain_positions_local, pair_width)
        ).astype(jnp.bfloat16)

    contact_matrix = lax.map(
        outer_rows,
        (starts, contact_matrix.reshape(row_blocks, 8, chain_positions_local, pair_width)),
    ).reshape(rows_dev, chain_positions_local, pair_width)
    bias_weight = mixing_logit_matrix[0]

    def norm_rows(pair_rows):
        normed_rows = standardize_features(pair_rows).astype(jnp.bfloat16)
        logit_rows = jnp.dot(
            normed_rows.reshape(8 * chain_positions_local, pair_width),
            bias_weight,
            preferred_element_type=jnp.float32,
        )
        return (normed_rows, logit_rows.reshape(8, chain_positions_local, head_count))

    pair_normed, logits = lax.map(
        norm_rows, contact_matrix.reshape(row_blocks, 8, chain_positions_local, pair_width)
    )
    logits = jnp.where(
        res_valid[None, :, None],
        logits.reshape(rows_dev, chain_positions_local, head_count),
        MASKED,
    )
    logits = logits.transpose(0, 2, 1)
    peak = of_everyone(jnp.max(logits, axis=2), "col")
    expo = jnp.exp(logits - peak[:, :, None])
    totals = over_copies(jnp.sum(expo, axis=2), "col")
    local_weights = (expo / totals[:, :, None]).astype(jnp.bfloat16)
    part_rows = rows_dev // lax.axis_size("row")
    sectioned = local_weights.reshape(1, rows_dev, head_count, 1, chain_positions_local)
    moved = lax.all_to_all(
        lax.all_to_all(sectioned, "row", split_axis=1, concat_axis=0, tiled=True),
        "col",
        split_axis=0,
        concat_axis=3,
        tiled=True,
    )
    moved = moved.reshape(
        ratio, part_rows, head_count, lax.axis_size("col") * chain_positions_local
    )
    mine = gather_directly(moved, "row", 1).reshape(
        chain_positions_local, head_count, lax.axis_size("col") * chain_positions_local
    )
    value_weight = mixing_value_gate_matrix[0][:, :hidden_width]
    gate_weight = mixing_value_gate_matrix[0][:, hidden_width:]
    gate = jax.nn.sigmoid(
        jnp.dot(reshaped_tensor, gate_weight, preferred_element_type=jnp.float32)
    ).reshape(homolog_rows_local, chain_positions_local, hidden_width)
    values_local = jnp.dot(reshaped_tensor, value_weight, preferred_element_type=jnp.float32)
    values_local = values_local.astype(jnp.bfloat16).reshape(
        homolog_rows_local, chain_positions_local, hidden_width
    )
    values_piece = lax.all_gather(values_local, "col", axis=1, tiled=True)
    count = values_piece.shape[1]
    heads_piece = values_piece.reshape(homolog_rows_local, count, head_count, head_width)
    averaged = jnp.einsum("ihj,sjhc->sihc", mine, heads_piece, preferred_element_type=jnp.float32)
    gated = (
        gate * averaged.reshape(homolog_rows_local, chain_positions_local, hidden_width)
    ).astype(jnp.bfloat16)
    contact_increment = jnp.dot(
        gated.reshape(homolog_rows_local * chain_positions_local, hidden_width),
        mixing_final_matrix[0],
        preferred_element_type=jnp.float32,
    )
    homolog_matrix = (
        homolog_matrix.astype(jnp.float32)
        + contact_increment.reshape(homolog_rows_local, chain_positions_local, homolog_rows_full)
    ).astype(jnp.bfloat16)
    up_weight = feedforward_gate_expand[0]
    down_weight = feedforward_shrink_matrix[0]

    def transition_rows(inputs):
        pair_rows, normed_rows = inputs
        hidden = jnp.dot(
            normed_rows.reshape(8 * chain_positions_local, pair_width),
            up_weight,
            preferred_element_type=jnp.float32,
        )
        active = (jax.nn.silu(hidden[:, :trans_width]) * hidden[:, trans_width:]).astype(
            jnp.bfloat16
        )
        update = jnp.dot(active, down_weight, preferred_element_type=jnp.float32)
        return (
            pair_rows.astype(jnp.float32) + update.reshape(8, chain_positions_local, pair_width)
        ).astype(jnp.bfloat16)

    contact_matrix = lax.map(
        transition_rows,
        (contact_matrix.reshape(row_blocks, 8, chain_positions_local, pair_width), pair_normed),
    )
    contact_matrix = contact_matrix.reshape(rows_dev, chain_positions_local, pair_width)
    return (homolog_matrix, contact_matrix)


def solution(mesh):
    in_specs = (
        P("row", "col", None),
        P("row", "col", None),
        P(),
        P(),
        P(),
        P(),
        P(),
        P(),
        P(),
        P(),
        P(),
    )
    out_specs = (P("row", "col", None), P("row", "col", None))
    return jax.shard_map(local, mesh=mesh, in_specs=in_specs, out_specs=out_specs, check_vma=False)
```

profile of v0, /device:TPU:32, one launch (start us, length us, event | category | flops | bytes accessed | tf_op | source)
XLA Modules:
  0.0 403.6 jit_solution(8511673040539516351)
XLA Ops:
  8.5 0.9 convert_reduce_fusion.1
  9.5 1.0 fusion.45
  10.5 0.9 fusion.46
  11.5 0.9 fusion.39
  12.9 40.2 %all_to_all.47 = bf16[16,8,5120]{2,1,0:T(8,128)(2,1)} all-to-all(bf16[16,8,5120]{2,1,0:T(8,128)(2,1)S(1)} %broadcast_in_dim.40), channel_id=1, replica_groups=mesh['row'=16,'col'=16] {'row'}, dimensions={0} | all-to-all | bytes 2621440 | tf_op jit(solution)/shard_map/all_to_all | solution.py:18
  53.1 3.3 reshape_reshape.3
  56.4 3.2 fusion.53
  59.7 4.4 %copy.88 = bf16[128,80,32]{0,2,1:T(8,128)(2,1)S(1)} copy(bf16[128,80,32]{2,1,0:T(8,128)(2,1)} %get-tuple-element.149) | data formatting | bytes 1310720 | tf_op jit(solution)/shard_map/slice | solution.py:98
  64.1 1.1 copy.89
  67.0 3.6 copy.91
  70.6 117.3 %all-gather.5.cloned.1.call-done = bf16[16,128,2560]{2,1,0:T(8,128)(2,1)} async-done(((bf16[1,128,2560]{2,1,0:T(8,128)(2,1)}), bf16[16,128,2560]{2,1,0:T(8,128)(2,1)}) %all-gather.5.cloned.1.call-update) | async-done | bytes 10485776 | tf_op jit(solution)/shard_map/all_gather | solution.py:28
  188.0 1.1 constant_dynamic-slice_fusion.2
  190.0 77.5 %while.32 = (s32[]{:T(128)}, bf16[10,8,80,128]{3,2,1,0:T(8,128)(2,1)S(1)}, bf16[10,8,80,128]{3,2,1,0:T(8,128)(2,1)}, s32[10]{0:T(128)S(1)}, bf16[128,80,32]{0,2,...) while((s32[]{:T(128)}, ...), condition=%wide.region_3.4_spmd, body=%wide.region_2.3_spmd.sunk | while | flops 337100800 | bytes 15212199 | solution.py:126
  193.3 2.4 copy.125
  196.1 1.7 fusion.86
  201.1 2.4 copy.125
  203.8 1.7 fusion.86
  208.8 2.4 copy.125
  211.6 1.7 fusion.86
  216.6 2.4 copy.125
  219.3 1.7 fusion.86
  224.3 2.4 copy.125
  227.1 1.7 fusion.86
  232.1 2.4 copy.125
  234.8 1.7 fusion.86
  239.8 2.4 copy.125
  242.6 1.7 fusion.86
  247.6 2.4 copy.125
  250.3 1.7 fusion.86
  255.3 2.4 copy.125
  258.1 1.7 fusion.86
  263.1 2.4 copy.125
  265.8 1.7 fusion.86
  267.6 1.4 broadcast.151.clone
  269.1 17.8 %while.33 = (s32[]{:T(128)}, bf16[10,8,80,128]{3,2,1,0:T(8,128)(2,1)}, f32[10,8,80,8]{2,3,1,0:T(8,128)S(1)}, bf16[10,8,80,128]{3,2,1,0:T(8,128)(2,1)S(1)}, bf16[128,8]{0,1:T(8,128)(2,1)S(1)}, /*index=5*/s32[]{:T(128)}) while((s32[]{:T(128)}, bf16[10,8,80,128]{3,2,1,0:T(8,128)(2,1)}, f32[10,8,80,8]{2,3,1,0:T(8,128)S(1)}, ...), condition=%wide.region_7.8_spmd, body=%wide.region_4.7_spmd.sunk | while | flops 2458242 | bytes 886861 | solution.py:141
  269.6 0.9 fusion.90
  273.1 0.9 fusion.90
  274.9 0.9 fusion.90
  280.2 0.9 fusion.90
  283.8 0.9 fusion.90
  285.6 0.9 fusion.90
  287.1 13.0 %all_to_all.48 = f32[16,80,8]{1,2,0:T(8,128)S(1)} all-to-all(f32[16,80,8]{1,2,0:T(8,128)S(1)} %broadcast_in_dim.66), channel_id=1, replica_groups=mesh['row'=16,'col'=16] {'col'}, dimensions={0} | all-to-all | bytes 81920 | tf_op jit(solution)/shard_map/all_to_all | solution.py:18
  300.6 12.6 %all_to_all.49 = f32[16,80,8]{1,2,0:T(8,128)S(1)} all-to-all(f32[16,80,8]{1,2,0:T(8,128)S(1)} %broadcast_in_dim.67), channel_id=1, replica_groups=mesh['row'=16,'col'=16] {'col'}, dimensions={0} | all-to-all | bytes 81920 | tf_op jit(solution)/shard_map/all_to_all | solution.py:18
  313.6 15.2 %all_to_all.50 = bf16[1,80,8,1,80]{4,2,3,0,1:T(8,128)(2,1)} all-to-all(bf16[1,80,8,1,80]{4,2,3,0,1:T(8,128)(2,1)S(1)} %fusion.47), channel_id=1, replica_groups=mesh['row'=16,'col'=16] {'row'}, dimensions={1} | all-to-all | bytes 204800 | tf_op jit(solution)/shard_map/all_to_all | solution.py:157
  328.8 3.5 all-to-all-start.4
  332.3 8.6 %copy.85 = bf16[8,1280,256]{1,2,0:T(8,128)(2,1)} copy(bf16[8,1280,256]{2,0,1:T(8,128)(2,1)} %all-gather.3.cloned.1.call-done) | data formatting | bytes 10485760 | tf_op jit(solution)/shard_map/all_gather | solution.py:178
  341.0 4.0 all-to-all-done.4
  345.2 1.3 broadcast_in_dim.69
  346.5 4.4 %all-to-all-start.5 = ((bf16[16,1,5,8,1280]{4,3,2,1,0:T(8,128)(2,1)}), bf16[16,1,5,8,1280]{4,3,2,1,0:T(8,128)(2,1)}, u32[]{:S(2)}, u32[]{:S(2)}) async-start(bf16[16,1,5,8,1280]{4,3,2,1,0:T(8,128)(2,1)} %broadcast_in_dim.69), calls=%async_computation.5 | async-start | bytes 3276800 | tf_op jit(solution)/shard_map/all_to_all | solution.py:18
  351.0 1.4 broadcast.151
  352.4 26.3 %while.34 = (s32[]{:T(128)}, bf16[10,8,80,128]{3,2,1,0:T(8,128)(2,1)}, bf16[10,8,80,128]{3,2,1,0:T(8,128)(2,1)S(1)}, bf16[10,8,80,128]{3,2,1,0:T(8,128)(2,1)}, b...) while((s32[]{:T(128)}, bf16[10,8,80,128]{3,2,1,0:T(8,128)(2,1)}, ...), condition=%wide.region_13.14_spmd, body=%wide.region_12.13_spmd.sunk | while | flops 253870080 | bytes 7111249 | solution.py:212
  352.4 0.9 constant_dynamic-slice_fusion.6
  355.0 0.9 constant_dynamic-slice_fusion.6
  357.7 0.9 constant_dynamic-slice_fusion.6
  360.3 0.9 constant_dynamic-slice_fusion.6
  362.9 0.9 constant_dynamic-slice_fusion.6
  365.5 0.9 constant_dynamic-slice_fusion.6
  368.2 0.9 constant_dynamic-slice_fusion.6
  370.8 0.9 constant_dynamic-slice_fusion.6
  373.4 0.9 constant_dynamic-slice_fusion.6
  376.0 0.9 constant_dynamic-slice_fusion.6
  378.7 10.6 %all-to-all-done.5 = bf16[16,1,5,8,1280]{4,3,2,1,0:T(8,128)(2,1)} async-done(((bf16[16,1,5,8,1280]{4,3,2,1,0:T(8,128)(2,1)}), bf16[16,1,5,8,1280]{4,3,2,1,0:T(8,128)(2,1)}, u32[]{:S(2)}, u32[]{:S(2)}) %all-to-all-start.5) | async-done | bytes 1638432 | tf_op jit(solution)/shard_map/all_to_all | solution.py:18
  389.2 4.5 %fusion.29 = f32[8,80,8,32]{1,3,0,2:T(8,128)S(1)} fusion(bf16[80,8,1280,1]{2,1,0,3:T(8,128)(2,1)} %bitcast.41, bf16[8,1280,8,32]{1,3,2,0:T(8,128)(2,1)} %bitcast.170), kind=kOutput, calls=%fused_computation.40 | convolution fusion | flops 419430400 | bytes 7536640 | tf_op jit(solution)/shard_map/ihj,sjhc->sihc/dot_general | solution.py:181
  395.8 0.9 fusion.40
  (182 shorter events, 52.3 us)
Async XLA Ops:
  7.2 388.1 %copy-start = (bf16[1,256,64]{1,2,0:T(8,128)(2,1)S(1)}, bf16[1,256,64]{1,2,0:T(8,128)(2,1)}, u32[]{:S(2)}) copy-start(bf16[1,256,64]{1,2,0:T(8,128)(2,1)} %param.25) | copy-start | bytes 98308
  7.2 180.8 %all-gather.5.cloned.1.call-start = ((), (), s32[]{:S(2)}) async-start(), calls=%async_computation.7 | async-start | bytes 11141120 | tf_op jit(solution)/shard_map/all_gather | solution.py:28
  64.0 1.4 copy-start.6
  65.1 1.9 copy-start.1
  65.2 267.2 %all-gather.3.cloned.1.call-start = ((), (), s32[]{:S(2)}) async-start(), calls=%async_computation.6 | async-start | bytes 5570560 | tf_op jit(solution)/shard_map/all_gather | solution.py:178
  189.1 1.0 copy-start.2
  267.6 1.5 copy-start.4
  267.6 1.5 copy-start.8
  328.8 16.2 %all-to-all-start.4 = ((bf16[16,5,8,1,80]{4,2,1,3,0:T(8,128)(2,1)}), bf16[16,5,8,1,80]{4,2,1,3,0:T(8,128)(2,1)S(1)}, u32[]{:S(2)}, u32[]{:S(2)}) async-start(bf16[16,5,8,1,80]{4,2,1,3,0:T(8,128)(2,1)} %bitcast.37), calls=%async_computation.4 | async-start | bytes 327680 | tf_op jit(solution)/shard_map/all_to_all | solution.py:156
  346.5 42.7 %all-to-all-start.5 = ((bf16[16,1,5,8,1280]{4,3,2,1,0:T(8,128)(2,1)}), bf16[16,1,5,8,1280]{4,3,2,1,0:T(8,128)(2,1)}, u32[]{:S(2)}, u32[]{:S(2)}) async-start(bf16[16,1,5,8,1280]{4,3,2,1,0:T(8,128)(2,1)} %broadcast_in_dim.69), calls=%async_computation.5 | async-start | bytes 3276800 | tf_op jit(solution)/shard_map/all_to_all | solution.py:18
  351.0 1.4 copy-start.3
  351.0 1.4 copy-start.7
  394.9 0.9 copy-start.5
Sparse Core Ops, SparseCore 0:
  65.3 122.6 all-gather.4
  190.6 79.4 all-gather.2
where the time goes:
time: 405 us; the launch traced here: 404 us
  waiting for transfers between devices  132 us (33%)
  blocking collectives  81.1 us (20%)
  local copies, waits for them, and re-layouts  73.5 us (18%)
  matrix products  44.7 us (11%)
  other arithmetic  28.4 us (7%)
  loops' own time  20.3 us (5%)
  between operations  15.7 us (4%)
  starting transfers between devices  8.03 us (2%)
    all_gather x1, waiting for transfers between devices, picked(): lax.all_gather(value, axis)  117 us
    all_to_all x3, blocking collectives, from_everyone(): lax.all_to_all(jnp.broadcast_to(value[None], (count, *value.shape)), axis...  65.9 us
    transpose x10, local copies, waits for them, and re-layouts, outer_rows(): product.reshape(8, outer_width, chain_positions_local, outer_width)  23.8 us
    another operation x1, loops' own time, local(): lax.map(outer_rows, (starts, contact_matrix.reshape(row_blocks, 8, chain_...  19.9 us
    dot_general x10, matrix products, outer_rows(): jnp.dot(outer.reshape(8 * chain_positions_local, outer_width * outer_widt...  17.1 us
    dynamic_update_slice x20, other arithmetic, local(): lax.map(outer_rows, (starts, contact_matrix.reshape(row_blocks, 8, chain_...  16.3 us
    all_to_all x1, blocking collectives, local(): lax.all_to_all(sectioned, 'row', split_axis=1, concat_axis=0, tiled=True)  15.2 us
    dynamic_slice x20, local copies, waits for them, and re-layouts, local(): lax.map(outer_rows, (starts, contact_matrix.reshape(row_blocks, 8, chain_...  15.1 us
  transfers between devices with their start and end apart: 4, of which 3 were waited for; matrix products, arithmetic and copies ran while one was open for 30% of the time, Pallas kernels for 0%

commit v1 on v0

--- a/solution.py
+++ b/solution.py
@@ -175,7 +175,9 @@
     values_local = values_local.astype(jnp.bfloat16).reshape(
         homolog_rows_local, chain_positions_local, hidden_width
     )
-    values_piece = lax.all_gather(values_local, "col", axis=1, tiled=True)
+    values_piece = jnp.concatenate(
+        lax.all_to_all(jnp.stack([values_local] * lax.axis_size("col")), "col", 0, 0), axis=1
+    )
     count = values_piece.shape[1]
     heads_piece = values_piece.reshape(homolog_rows_local, count, head_count, head_width)
     averaged = jnp.einsum("ihj,sjhc->sihc", mine, heads_piece, preferred_element_type=jnp.float32)

time: 405 us -> 554 us (1.37)
  waiting for transfers between devices: 132 us -> 266 us
  blocking collectives: 81.1 us -> 57.7 us
  local copies, waits for them, and re-layouts: 73.5 us -> 93.4 us
  starting transfers between devices: 8.03 us -> 25 us
    all_to_all x0 -> x1, waiting for transfers between devices: none -> 117 us  [local(): lax.all_to_all(jnp.stack([values_local] * lax.axis_size('col')), 'col', 0...]
    all_to_all x3 -> x1, blocking collectives: 65.9 us -> 40.2 us  [from_everyone(): lax.all_to_all(jnp.broadcast_to(value[None], (count, *value.shape)), axis...]
    all_to_all x1 -> x3, waiting for transfers between devices: 10.6 us -> 30.3 us  [from_everyone(): lax.all_to_all(jnp.broadcast_to(value[None], (count, *value.shape)), axis...]
    another operation x3 -> x5, local copies, waits for them, and re-layouts: 3.12 us -> 19.9 us  [the longest x1 14 us: local(): values_piece.reshape(homolog_rows_local, count, head_count, head_width)]
    reshape x1, local copies, waits for them, and re-layouts: 0.83 us -> 11.4 us  [local(): jnp.concatenate(lax.all_to_all(jnp.stack([values_local] * lax.axis_size('...]
    all_to_all x1 -> x3, starting transfers between devices: 4.43 us -> 13.3 us  [from_everyone(): lax.all_to_all(jnp.broadcast_to(value[None], (count, *value.shape)), axis...]
    all_gather x1 -> x0, local copies, waits for them, and re-layouts: 8.63 us -> none  [local(): values_piece = lax.all_gather(values_local, 'col', axis=1, tiled=True)]
  transfers between devices with their start and end apart: 4 -> 6, of which waited for: 3 -> 5; matrix products, arithmetic and copies ran while one was open for 30% -> 10% of each run, Pallas kernels for 0% -> 0%
where the time goes in v1:
time: 554 us; the launch traced here: 551 us
  waiting for transfers between devices  266 us (48%)
  local copies, waits for them, and re-layouts  93.4 us (17%)
  blocking collectives  57.7 us (10%)
  matrix products  44.7 us (8%)
  other arithmetic  28.2 us (5%)
  starting transfers between devices  25 us (5%)
  loops' own time  20.3 us (4%)
  between operations  15.7 us (3%)
    all_gather x1, waiting for transfers between devices, picked(): lax.all_gather(value, axis)  119 us
    all_to_all x1, waiting for transfers between devices, local(): lax.all_to_all(jnp.stack([values_local] * lax.axis_size('col')), 'col', 0...  117 us
    all_to_all x1, blocking collectives, from_everyone(): lax.all_to_all(jnp.broadcast_to(value[None], (count, *value.shape)), axis...  40.2 us
    all_to_all x3, waiting for transfers between devices, from_everyone(): lax.all_to_all(jnp.broadcast_to(value[None], (count, *value.shape)), axis...  30.3 us
    transpose x10, local copies, waits for them, and re-layouts, outer_rows(): product.reshape(8, outer_width, chain_positions_local, outer_width)  23.8 us
    another operation x1, loops' own time, local(): lax.map(outer_rows, (starts, contact_matrix.reshape(row_blocks, 8, chain_...  19.9 us
    all_to_all x1, blocking collectives, local(): lax.all_to_all(sectioned, 'row', split_axis=1, concat_axis=0, tiled=True)  17.5 us
    dot_general x10, matrix products, outer_rows(): jnp.dot(outer.reshape(8 * chain_positions_local, outer_width * outer_widt...  17 us
  transfers between devices with their start and end apart: 6, of which 5 were waited for; matrix products, arithmetic and copies ran while one was open for 10% of the time, Pallas kernels for 0%

profile of v1, /device:TPU:32, one launch (start us, length us, event | category | flops | bytes accessed | tf_op | source)
XLA Modules:
  0.0 551.3 jit_solution(18102811643343637259)
XLA Ops:
  8.5 0.9 convert_reduce_fusion.1
  9.5 1.0 fusion.45
  10.5 0.9 fusion.46
  11.5 0.9 fusion.39
  12.9 40.2 %all_to_all.52 = bf16[16,8,5120]{2,1,0:T(8,128)(2,1)} all-to-all(bf16[16,8,5120]{2,1,0:T(8,128)(2,1)S(1)} %broadcast_in_dim.40), channel_id=1, replica_groups=mesh['row'=16,'col'=16] {'row'}, dimensions={0} | all-to-all | bytes 2621440 | tf_op jit(solution)/shard_map/all_to_all | solution.py:18
  53.1 3.3 reshape_reshape.7
  56.4 3.3 fusion.53
  59.7 4.5 copy.85
  64.2 1.1 copy.86
  65.5 3.6 copy.88
  69.1 119.0 %all-gather.2.cloned.1.call-done = bf16[16,128,2560]{2,1,0:T(8,128)(2,1)} async-done(((bf16[1,128,2560]{2,1,0:T(8,128)(2,1)}), bf16[16,128,2560]{2,1,0:T(8,128)(2,1)}) %all-gather.2.cloned.1.call-update) | async-done | bytes 10485776 | tf_op jit(solution)/shard_map/all_gather | solution.py:28
  188.1 1.1 constant_dynamic-slice_fusion.2
  190.2 77.5 %while.32 = (s32[]{:T(128)}, bf16[10,8,80,128]{3,2,1,0:T(8,128)(2,1)S(1)}, bf16[10,8,80,128]{3,2,1,0:T(8,128)(2,1)}, s32[10]{0:T(128)S(1)}, bf16[128,80,32]{0,2,...) while((s32[]{:T(128)}, ...), condition=%wide.region_3.4_spmd, body=%wide.region_2.3_spmd.sunk | while | flops 337100800 | bytes 15212207 | solution.py:126
  193.5 2.4 copy.122
  196.2 1.7 fusion.86
  201.3 2.4 copy.122
  204.0 1.7 fusion.86
  209.0 2.4 copy.122
  211.7 1.7 fusion.86
  216.8 2.4 copy.122
  219.5 1.7 fusion.86
  224.5 2.4 copy.122
  227.2 1.7 fusion.86
  232.2 2.4 copy.122
  235.0 1.7 fusion.86
  240.0 2.4 copy.122
  242.7 1.7 fusion.86
  247.7 2.4 copy.122
  250.5 1.7 fusion.86
  255.5 2.4 copy.122
  258.2 1.7 fusion.86
  263.2 2.4 copy.122
  266.0 1.7 fusion.86
  267.7 1.4 broadcast.152.clone
  269.1 17.7 %while.33 = (s32[]{:T(128)}, bf16[10,8,80,128]{3,2,1,0:T(8,128)(2,1)}, f32[10,8,80,8]{2,3,1,0:T(8,128)S(1)}, bf16[10,8,80,128]{3,2,1,0:T(8,128)(2,1)S(1)}, bf16[128,8]{0,1:T(8,128)(2,1)S(1)}, /*index=5*/s32[]{:T(128)}) while((s32[]{:T(128)}, bf16[10,8,80,128]{3,2,1,0:T(8,128)(2,1)}, f32[10,8,80,8]{2,3,1,0:T(8,128)S(1)}, ...), condition=%wide.region_7.8_spmd, body=%wide.region_4.7_spmd.sunk | while | flops 2458242 | bytes 886361 | solution.py:141
  275.3 0.9 fusion.90
  287.7 3.5 all-to-all-start.2
  291.5 9.8 %all-to-all-done.2 = f32[16,80,8]{1,2,0:T(8,128)S(1)} async-done(((f32[16,80,8]{1,2,0:T(8,128)}), f32[16,80,8]{1,2,0:T(8,128)S(1)}, u32[]{:S(2)}, u32[]{:S(2)}) %all-to-all-start.2) | async-done | bytes 40992 | tf_op jit(solution)/shard_map/all_to_all | solution.py:18
  302.3 3.7 all-to-all-start.3
  306.3 9.7 %all-to-all-done.3 = f32[16,80,8]{1,2,0:T(8,128)S(1)} async-done(((f32[16,80,8]{1,2,0:T(8,128)}), f32[16,80,8]{1,2,0:T(8,128)S(1)}, u32[]{:S(2)}, u32[]{:S(2)}) %all-to-all-start.3) | async-done | bytes 40992 | tf_op jit(solution)/shard_map/all_to_all | solution.py:18
  316.0 2.8 stack.3
  318.8 4.6 all-to-all-start
  323.8 117.0 %all-to-all-done = bf16[16,8,80,256]{3,2,1,0:T(8,128)(2,1)} async-done(((bf16[16,8,80,256]{3,2,1,0:T(8,128)(2,1)}), bf16[16,8,80,256]{3,2,1,0:T(8,128)(2,1)}, u32[]{:S(2)}, u32[]{:S(2)}) %all-to-all-start) | async-done | bytes 5242912 | tf_op jit(solution)/shard_map/all_to_all | solution.py:179
  440.8 17.5 %all_to_all.53 = bf16[1,80,8,1,80]{4,2,3,0,1:T(8,128)(2,1)} all-to-all(bf16[1,80,8,1,80]{4,2,3,0,1:T(8,128)(2,1)S(1)} %fusion.47), channel_id=1, replica_groups=mesh['row'=16,'col'=16] {'row'}, dimensions={1} | all-to-all | bytes 204800 | tf_op jit(solution)/shard_map/all_to_all | solution.py:157
  458.3 7.1 %all-to-all-start.5 = ((bf16[16,5,8,1,80]{4,2,1,3,0:T(8,128)(2,1)}), bf16[16,5,8,1,80]{4,2,1,3,0:T(8,128)(2,1)S(1)}, u32[]{:S(2)}, u32[]{:S(2)}) async-start(bf16[16,5,8,1,80]{4,2,1,3,0:T(8,128)(2,1)} %bitcast.37), calls=%async_computation.5 | async-start | bytes 327680 | tf_op jit(solution)/shard_map/all_to_all | solution.py:156
  465.4 11.4 %copy.82 = bf16[8,16,80,256]{2,1,3,0:T(8,128)(2,1)} copy(bf16[8,16,80,256]{3,2,0,1:T(8,128)(2,1)} %bitcast.22) | data formatting | bytes 10485760 | tf_op jit(solution)/shard_map/reshape | solution.py:178
  476.8 14.0 %reshape_reshape.6 = bf16[8,1280,8,32]{1,3,2,0:T(8,128)(2,1)} reshape(bf16[8,16,80,256]{2,1,3,0:T(8,128)(2,1)} %copy.82) | data formatting | bytes 10485760 | tf_op jit(solution)/shard_map/reshape;reshape | solution.py:182
  491.1 1.3 broadcast_in_dim.69
  492.4 6.1 %all-to-all-start.6 = ((bf16[16,1,5,8,1280]{4,3,2,1,0:T(8,128)(2,1)}), bf16[16,1,5,8,1280]{4,3,2,1,0:T(8,128)(2,1)}, u32[]{:S(2)}, u32[]{:S(2)}) async-start(bf16[16,1,5,8,1280]{4,3,2,1,0:T(8,128)(2,1)} %broadcast_in_dim.69), calls=%async_computation.6 | async-start | bytes 3276800 | tf_op jit(solution)/shard_map/all_to_all | solution.py:18
  498.5 1.4 broadcast.152
  499.9 26.3 %while.34 = (s32[]{:T(128)}, bf16[10,8,80,128]{3,2,1,0:T(8,128)(2,1)}, bf16[10,8,80,128]{3,2,1,0:T(8,128)(2,1)S(1)}, bf16[10,8,80,128]{3,2,1,0:T(8,128)(2,1)}, b...) while((s32[]{:T(128)}, bf16[10,8,80,128]{3,2,1,0:T(8,128)(2,1)}, ...), condition=%wide.region_13.14_spmd, body=%wide.region_12.13_spmd.sunk | while | flops 253870080 | bytes 7110749 | solution.py:214
  499.9 0.9 constant_dynamic-slice_fusion.6
  502.5 0.9 constant_dynamic-slice_fusion.6
  505.2 0.9 constant_dynamic-slice_fusion.6
  507.8 0.9 constant_dynamic-slice_fusion.6
  510.4 0.9 constant_dynamic-slice_fusion.6
  513.0 0.9 constant_dynamic-slice_fusion.6
  515.7 0.9 constant_dynamic-slice_fusion.6
  518.3 0.9 constant_dynamic-slice_fusion.6
  520.9 0.9 constant_dynamic-slice_fusion.6
  523.5 0.9 constant_dynamic-slice_fusion.6
  526.2 10.8 %all-to-all-done.6 = bf16[16,1,5,8,1280]{4,3,2,1,0:T(8,128)(2,1)} async-done(((bf16[16,1,5,8,1280]{4,3,2,1,0:T(8,128)(2,1)}), bf16[16,1,5,8,1280]{4,3,2,1,0:T(8,128)(2,1)}, u32[]{:S(2)}, u32[]{:S(2)}) %all-to-all-start.6) | async-done | bytes 1638432 | tf_op jit(solution)/shard_map/all_to_all | solution.py:18
  536.9 4.5 fusion.29
  543.5 0.9 fusion.40
  (184 shorter events, 56.9 us)
Async XLA Ops:
  7.2 535.9 %copy-start = (bf16[1,256,64]{1,2,0:T(8,128)(2,1)S(1)}, bf16[1,256,64]{1,2,0:T(8,128)(2,1)}, u32[]{:S(2)}) copy-start(bf16[1,256,64]{1,2,0:T(8,128)(2,1)} %param.25) | copy-start | bytes 98308
  7.2 181.0 %all-gather.2.cloned.1.call-start = ((), (), s32[]{:S(2)}) async-start(), calls=%async_computation.7 | async-start | bytes 11141120 | tf_op jit(solution)/shard_map/all_gather | solution.py:28
  59.7 5.7 %copy-start.1 = (bf16[128,80,32]{2,1,0:T(8,128)(2,1)S(1)}, bf16[128,80,32]{2,1,0:T(8,128)(2,1)}, u32[]{:S(2)}) copy-start(bf16[128,80,32]{2,1,0:T(8,128)(2,1)} %get-tuple-element.148) | copy-start | bytes 1966084
  189.3 1.0 copy-start.2
  267.7 1.4 copy-start.4
  267.7 1.4 copy-start.8
  286.8 19.2 %copy-start.6 = (bf16[1,64,512]{2,1,0:T(8,128)(2,1)S(1)}, bf16[1,64,512]{2,1,0:T(8,128)(2,1)}, u32[]{:S(2)}) copy-start(bf16[1,64,512]{2,1,0:T(8,128)(2,1)} %param.23) | copy-start | bytes 196612
  287.7 13.5 %all-to-all-start.2 = ((f32[16,80,8]{1,2,0:T(8,128)}), f32[16,80,8]{1,2,0:T(8,128)S(1)}, u32[]{:S(2)}, u32[]{:S(2)}) async-start(f32[16,80,8]{1,2,0:T(8,128)} %broadcast_in_dim.66), calls=%async_computation.2 | async-start | bytes 131072 | tf_op jit(solution)/shard_map/all_to_all | solution.py:18
  302.3 13.7 %all-to-all-start.3 = ((f32[16,80,8]{1,2,0:T(8,128)}), f32[16,80,8]{1,2,0:T(8,128)S(1)}, u32[]{:S(2)}, u32[]{:S(2)}) async-start(f32[16,80,8]{1,2,0:T(8,128)} %broadcast_in_dim.67), calls=%async_computation.3 | async-start | bytes 131072 | tf_op jit(solution)/shard_map/all_to_all | solution.py:18
  318.8 122.0 %all-to-all-start = ((bf16[16,8,80,256]{3,2,1,0:T(8,128)(2,1)}), bf16[16,8,80,256]{3,2,1,0:T(8,128)(2,1)}, u32[]{:S(2)}, u32[]{:S(2)}) async-start(bf16[16,8,80,256]{3,2,1,0:T(8,128)(2,1)} %stack.3), calls=%async_computation | async-start | bytes 10485760 | tf_op jit(solution)/shard_map/all_to_all | solution.py:179
  458.3 32.5 %all-to-all-start.5 = ((bf16[16,5,8,1,80]{4,2,1,3,0:T(8,128)(2,1)}), bf16[16,5,8,1,80]{4,2,1,3,0:T(8,128)(2,1)S(1)}, u32[]{:S(2)}, u32[]{:S(2)}) async-start(bf16[16,5,8,1,80]{4,2,1,3,0:T(8,128)(2,1)} %bitcast.37), calls=%async_computation.5 | async-start | bytes 327680 | tf_op jit(solution)/shard_map/all_to_all | solution.py:156
  492.4 44.6 %all-to-all-start.6 = ((bf16[16,1,5,8,1280]{4,3,2,1,0:T(8,128)(2,1)}), bf16[16,1,5,8,1280]{4,3,2,1,0:T(8,128)(2,1)}, u32[]{:S(2)}, u32[]{:S(2)}) async-start(bf16[16,1,5,8,1280]{4,3,2,1,0:T(8,128)(2,1)} %broadcast_in_dim.69), calls=%async_computation.6 | async-start | bytes 3276800 | tf_op jit(solution)/shard_map/all_to_all | solution.py:18
  498.5 1.4 copy-start.3
  498.5 1.4 copy-start.7
  542.6 0.9 copy-start.5
Sparse Core Ops, SparseCore 0:
  65.5 122.6 all-gather.1
